TPU v7x, 32 devices: a whole 2x2x4 slice. The times are simulated.
32 devices in a mesh: tm: 16 (over z, y, core), space: 2 (over x).
Axes of the slice: x: 2, y: 2, z: 4, core: 2. Of those that a mesh axis runs over, the one named last changes fastest.
Arguments:
- cpoint_guess: float32 [16, 3, 32, 1024], P('tm', None, 'space'), may hold values from -6 to 6
- tide_forcing: float32 [128, 3, 32, 1024], P('tm', None, 'space'), may hold values from -4 to 4
- depth: float32 [32, 1024], P('space'), may hold values from 0.5 to 1.5
- drag: float32 [32, 1024], P('space'), may hold values from 0.01 to 0.08
Outputs:
- improved: float32 [128, 3, 32, 1024], P('tm', None, 'space')
- cpoint_residual: float32 [16, 3, 32, 1024], P('tm', None, 'space')
All inputs are finite; a program needn't handle non-finite values.
Results may differ from a plain program's by a relative error of at most 0.0003.
Values sent between devices are 32-bit elements; how exact they have to be, the bound alone decides.
A program may use at most 128 MiB of HBM per device.

v0:
```python
import jax
import jax.numpy as jnp
from jax import lax
from jax.experimental import pallas as pl
from jax.experimental.pallas import tpu as pltpu
from jax.sharding import PartitionSpec as P

LEVELS = 5


coriolis = 0.1
fine_courant = 0.25
coarse_courant = 0.5


def with_halo(cells, sides, width):
    for axis, dim in sides:
        count = lax.axis_size(axis)
        head = lax.slice_in_dim(cells, 0, width, axis=dim)
        tail = lax.slice_in_dim(cells, cells.shape[dim] - width, cells.shape[dim], axis=dim)
        cells = jnp.concatenate(
            [
                lax.ppermute(tail, axis, [(i, (i + 1) % count) for i in range(count)]),
                cells,
                lax.ppermute(head, axis, [((i + 1) % count, i) for i in range(count)]),
            ],
            axis=dim,
        )
    return cells


def shifted(block, axis, distance):
    devices = range(lax.axis_size(axis))
    route = [((i - distance) % len(devices), i) for i in devices]
    return lax.ppermute(block, axis, route)


def across_rows(field):
    return (field[2:] - field[:-2]) * 0.5


def along_cols(field):
    return (jnp.roll(field, -1, -1) - jnp.roll(field, 1, -1)) * 0.5


def advance(padded, coefficients, courant):
    height = padded[0]
    eastward = padded[1]
    northward = padded[2]
    new_height = height[1:-1] - courant * coefficients[0, 1:-1] * (
        across_rows(eastward) + along_cols(northward)[1:-1]
    )
    retain = 1.0 - coefficients[1, 2:-2]
    east_middle = eastward[2:-2]
    north_middle = northward[2:-2]
    new_east = (
        retain * east_middle + courant * coriolis * north_middle - courant * across_rows(new_height)
    )
    new_north = (
        retain * north_middle
        - courant * coriolis * east_middle
        - courant * along_cols(new_height)[1:-1]
    )
    return jnp.stack((new_height[1:-1], new_east, new_north))


def body(cpoint_guess, tide_forcing, depth, drag):
    coefficients = with_halo(jnp.stack((depth, drag)), (("space", 1),), 4)
    narrow = coefficients[:, 2:-2]

    def one_substep(state, courant):
        padded = with_halo(state, (("space", 1),), 2)
        return advance(padded, narrow, courant)

    def fine_map(state):
        padded = with_halo(state, (("space", 1),), 4)
        middle = advance(padded, coefficients, fine_courant)
        result = advance(middle, narrow, fine_courant)
        return result

    def coarse_map(state):
        return one_substep(state, coarse_courant)

    def pass_on(state, stride, mapper):
        result = shifted(mapper(state), "tm", stride)
        return result

    start = cpoint_guess[0]
    state = start
    for moment in range(1, tide_forcing.shape[0]):
        state = fine_map(state) + tide_forcing[moment]
    right = pass_on(state, 1, fine_map) + tide_forcing[0] - start
    rights = [right]
    for level in range(1, LEVELS):
        current = rights[-1]
        rights.append(current + pass_on(current, 2 ** (level - 1), coarse_map))
    top_stride = 2 ** (LEVELS - 1)
    points = lax.axis_size("tm") // top_stride
    position = lax.axis_index("tm")
    base = rights[-1]
    anchor = position % top_stride == 0

    def sweep(counter, correction):
        arrived = pass_on(correction, top_stride, coarse_map)
        target = jnp.logical_and(anchor, position // top_stride == counter % points)
        return jnp.where(target, arrived + base, correction)

    correction = lax.fori_loop(1, points + 1, sweep, base)
    for level in range(LEVELS - 1, 0, -1):
        stride = 2 ** (level - 1)
        arrived = pass_on(correction, stride, coarse_map)
        odd_point = position % (2 * stride) == stride
        correction = jnp.where(odd_point, arrived + rights[level - 1], correction)
    state = start + correction
    states = [state]
    for moment in range(1, tide_forcing.shape[0]):
        state = fine_map(state) + tide_forcing[moment]
        states.append(state)
    return (jnp.stack(states), right[None])


lanes = 128
group = 4
height_scale = 0.125
early_edges = 3


def cycle_kernel(
    guess_hbm, forcing_hbm, depth_hbm, drag_hbm, out, residual,
    guess, forcing, raw, raw_in, fine_depth, coarse_depth, retain, track, mid, edges, edges_in,
    ahead, ahead_in, first, lift, lift_in, part, part_in, second, third, fourth, climb, wave,
    lower_in, lower, lower_here, own_in, passed, passed_in, relax, relax_mid,
    load_sems, coef_sems, ahead_sems, edge_send, edge_recv, lift_sems, part_send, part_recv,
    second_send, second_recv, third_send, third_recv, fourth_send, fourth_recv, relay_send,
    lower_send, lower_recv, here_sems, own_sems, passed_sems, wave_send, wave_recv, out_sems, go_sem,
):
    tm = lax.axis_index("tm")
    sp = lax.axis_index("space")
    count = lax.axis_size("tm")
    moments = forcing.shape[0]
    own = guess.shape[1]
    rows = 2 * own
    strips = guess.shape[2]
    chunks = rows // group
    other = 1 - sp
    odd = tm % 2
    chip = (tm // 2) % 2
    layer = tm // 4
    pair = layer % 2
    half = layer // 2
    before = (tm + count - 1) % count
    after_chip = (tm + 2) % count
    sibling = tm + 1 - 2 * odd
    facing = tm + 2 - 4 * chip
    beside = tm + 4 - 8 * pair
    inner = pair != half
    inward = (tm + 4 - 8 * half + count) % count

    def load(src, dst, index):
        return [
            pltpu.make_async_copy(
                src.at[..., pl.ds(strip * lanes, lanes)], dst.at[..., strip, :],
                load_sems.at[index, strip],
            )
            for strip in range(strips)
        ]

    loads = [
        load(depth_hbm, raw.at[0], 0),
        load(drag_hbm, raw.at[1], 1),
        load(guess_hbm.at[0], guess, 2),
        load(forcing_hbm.at[0], forcing.at[0], 3),
        load(forcing_hbm.at[1:moments], forcing.at[1:moments], 4),
    ]

    def remote(src, dst, send, recv, to):
        return pltpu.make_async_remote_copy(
            src_ref=src, dst_ref=dst, send_sem=send, recv_sem=recv,
            device_id=to, device_id_type=pl.DeviceIdType.MESH,
        )

    barrier = pltpu.get_barrier_semaphore()
    partners = [(tm, other)]
    for distance in (1, 2, 4):
        partners.append(((tm + distance) % count, sp))
        partners.append(((tm + count - distance) % count, sp))
    for to in partners:
        pl.semaphore_signal(barrier, inc=1, device_id=to, device_id_type=pl.DeviceIdType.MESH)
    for copies in loads:
        for copy in copies:
            copy.start()

    lane = lax.broadcasted_iota(jnp.int32, (1, strips, lanes), 2)

    def down_cols(a):
        here = lax.broadcasted_iota(jnp.int32, a.shape, 2)
        following = jnp.where(here == 0, pltpu.roll(a, strips - 1, 1), a)
        preceding = jnp.where(here == lanes - 1, pltpu.roll(a, 1, 1), a)
        return pltpu.roll(following, lanes - 1, 2) - pltpu.roll(preceding, 1, 2)

    def take(ref, start, size):
        total = ref.shape[0]
        start %= total
        if start + size <= total:
            return ref[start : start + size]
        return jnp.concatenate([ref[start:total], ref[0 : start + size - total]], axis=0)

    def raise_heights(h, u_before, u_after, v, depths):
        return h - depths * (u_after - u_before + down_cols(v))

    def new_speeds(u, v, h_before, h, h_after, kept, courant):
        turn = courant * coriolis
        east = h_after - h_before
        north = down_cols(h)
        slope = courant * 0.5 / height_scale
        if slope != 1.0:
            east = slope * east
            north = slope * north
        return kept * u + turn * v - east, kept * v - turn * u - north

    def fine_substep(src, dst):
        for r in range(0, rows, group):
            dst[0, r : r + group] = raise_heights(
                src[0, r : r + group], take(src.at[1], r - 1, group), take(src.at[1], r + 1, group),
                src[2, r : r + group], fine_depth[r : r + group],
            )
        for r in range(0, rows, group):
            east, north = new_speeds(
                src[1, r : r + group], src[2, r : r + group], take(dst.at[0], r - 1, group),
                dst[0, r : r + group], take(dst.at[0], r + 1, group), retain[r : r + group],
                fine_courant,
            )
            dst[1, r : r + group] = east
            dst[2, r : r + group] = north

    def fine(src, dst):
        fine_substep(src, mid)
        fine_substep(mid, dst)

    def coarse_rows(src, frame, row, size=group):
        start = row - frame
        h = raise_heights(
            take(src.at[0], start - 1, size + 2), take(src.at[1], start - 2, size + 2),
            take(src.at[1], start, size + 2), take(src.at[2], start - 1, size + 2),
            take(coarse_depth, row - 1, size + 2),
        )
        east, north = new_speeds(
            take(src.at[1], start, size), take(src.at[2], start, size), h[0:size],
            h[1 : size + 1], h[2 : size + 2], take(retain, row, size), coarse_courant,
        )
        return h[1 : size + 1], east, north

    def coarse(src, frame, dst, dst_frame, added=None, added_frame=0):
        for r in range(0, rows, group):
            values = coarse_rows(src, frame, r + dst_frame)
            for field in range(3):
                value = values[field]
                if added is not None:
                    value = value + take(added.at[field], r + dst_frame - added_frame, group)
                dst[field, r : r + group] = value

    for copies in loads[:2]:
        for copy in copies:
            copy.wait()
    pl.semaphore_wait(barrier, len(partners))
    coef_copy = remote(raw, raw_in, coef_sems.at[0], coef_sems.at[1], (tm, other))
    coef_copy.start()

    for copies in loads[2:4]:
        for copy in copies:
            copy.wait()

    def scaled(a):
        return jnp.concatenate([a[0:1] * height_scale, a[1:3]], axis=0)

    start_state = scaled(guess[...])
    ahead[...] = scaled(forcing[0]) - start_state
    ahead_copy = remote(ahead, ahead_in, ahead_sems.at[0], ahead_sems.at[1], (before, sp))
    ahead_copy.start()
    guess[...] = start_state
    track[0, :, 0:own] = start_state
    track[0, :, own:rows] = jnp.zeros((3, own, strips, lanes), jnp.float32)
    relax[0] = jnp.zeros((3, own, strips, lanes), jnp.float32)
    fine_depth[0:own] = (fine_courant * 0.5 * height_scale) * raw[0]
    coarse_depth[0:own] = (coarse_courant * 0.5 * height_scale) * raw[0]
    retain[0:own] = 1.0 - raw[1]
    for copy in loads[4]:
        copy.wait()
    coef_copy.wait()
    fine_depth[own:rows] = (fine_courant * 0.5 * height_scale) * raw_in[0]
    coarse_depth[own:rows] = (coarse_courant * 0.5 * height_scale) * raw_in[0]
    retain[own:rows] = 1.0 - raw_in[1]

    def edge_copy(moment):
        return remote(
            edges.at[moment], edges_in.at[moment], edge_send.at[moment], edge_recv.at[moment],
            (tm, other),
        )

    def propagate(moment, carry):
        previous = moment - 1
        src = track.at[previous]
        dst = track.at[moment]
        fine(src, dst)
        for index, (ref, field) in enumerate(((src, 1), (mid, 0), (mid, 1), (dst, 0))):
            edges[previous, 2 * index] = ref[field, 0]
            edges[previous, 2 * index + 1] = ref[field, own - 1]

        @pl.when(previous < early_edges)
        def _():
            edge_copy(previous).start()

        dst[0, 0:own] += height_scale * forcing[moment, 0]
        dst[1, 0:own] += forcing[moment, 1]
        dst[2, 0:own] += forcing[moment, 2]
        return carry

    lax.fori_loop(1, moments, propagate, 0)
    fine(track.at[moments - 1], first)
    ahead_copy.wait()
    first[:, 0:own] += ahead_in[...]

    def bounded(ref, start, size, above, below):
        if start < 0:
            return jnp.concatenate([above[None], ref[0 : start + size]], axis=0)
        if start + size > own:
            return jnp.concatenate([ref[start:own], below[None]], axis=0)
        return ref[start : start + size]

    def relax_substep(src, dst, border, base):
        u_below, u_above = border[base], border[base + 1]
        h_below, h_above = border[base + 2], border[base + 3]
        for r in range(0, own, group):
            dst[0, r : r + group] = raise_heights(
                src[0, r : r + group], bounded(src.at[1], r - 1, group, u_above, u_below),
                bounded(src.at[1], r + 1, group, u_above, u_below), src[2, r : r + group],
                fine_depth[r : r + group],
            )
        for r in range(0, own, group):
            east, north = new_speeds(
                src[1, r : r + group], src[2, r : r + group],
                bounded(dst.at[0], r - 1, group, h_above, h_below), dst[0, r : r + group],
                bounded(dst.at[0], r + 1, group, h_above, h_below), retain[r : r + group],
                fine_courant,
            )
            dst[1, r : r + group] = east
            dst[2, r : r + group] = north

    def relaxed(low, high):
        def step(moment, carry):
            previous = moment - 1
            edge_copy(previous).wait()
            border = edges_in.at[previous]
            a = previous % 2
            b = moment % 2
            relax_substep(relax.at[a], relax_mid, border, 0)
            relax_substep(relax_mid, relax.at[b], border, 4)
            track[moment, :, 0:own] += relax[b]
            return carry

        lax.fori_loop(low, high, step, 0)

    def late_edges():
        def step(moment, carry):
            edge_copy(moment).start()
            return carry

        lax.fori_loop(early_edges, moments - 1, step, 0)

    def span(index):
        return pl.ds(index * group, group)

    lift_copy = remote(lift, lift_in, lift_sems.at[0], lift_sems.at[1], (sibling, sp))
    here_copy = remote(lower, lower_here, here_sems.at[0], here_sems.at[1], (sibling, sp))
    own_copy = remote(
        second.at[chip, :, 0:own], own_in, own_sems.at[0], own_sems.at[1], (sibling, sp)
    )
    passed_copy = remote(passed, passed_in, passed_sems.at[0], passed_sems.at[1], (after_chip, sp))
    lower_copies = [
        remote(
            first.at[:, start : start + own], lower_in.at[:, own - start : rows - start],
            lower_send.at[index], lower_recv.at[1 - index], (tm, other),
        )
        for index, start in enumerate((0, own))
    ]
    top_frame = 4
    wave_copies = [
        remote(
            climb.at[1, :, start:end], wave.at[0, :, (start + top_frame) % rows : (end + top_frame - 1) % rows + 1],
            wave_send.at[index], wave_recv.at[index], (sibling, sp),
        )
        for index, (start, end) in enumerate(((0, own), (own, rows - top_frame), (rows - top_frame, rows)))
    ]

    def part_copy(index):
        landing = (index + chunks // 2) % chunks
        return remote(
            part.at[:, span(index)], part_in.at[:, span(landing)], part_send.at[index],
            part_recv.at[landing], (tm, other),
        )

    def exchange(ref, slot, send, recv, to):
        def copy(index):
            return remote(
                ref.at[slot, :, span(index)], ref.at[slot, :, span(index)], send.at[index],
                recv.at[index], (to, sp),
            )

        return copy

    second_copy = exchange(second, chip, second_send, second_recv, facing)
    second_in = exchange(second, 1 - chip, second_send, second_recv, facing)
    third_copy = exchange(third, pair, third_send, third_recv, beside)
    third_in = exchange(third, 1 - pair, third_send, third_recv, beside)
    fourth_copy = exchange(fourth, half, fourth_send, fourth_recv, inward)
    fourth_in = exchange(fourth, 1 - half, relay_send, fourth_recv, beside)

    @pl.when(odd == 0)
    def _():
        coarse(first, 0, lift, 0)
        lift_copy.start()
        relaxed(1, early_edges + 1)
        pl.semaphore_wait(go_sem, 1)
        late_edges()
        for copy in lower_copies:
            copy.start()
        relaxed(early_edges + 1, moments)
        own_copy.wait_recv()
        for copy in lower_copies:
            copy.wait()
        lower[...] = first[...] + lower_in[...]
        here_copy.start()
        for r in range(0, own, group):
            values = coarse_rows(lower, 0, r)
            for field in range(3):
                passed[field, r : r + group] = own_in[field, r : r + group] - values[field]
        passed_copy.start()
        lift_copy.wait_send()
        passed_copy.wait()
        here_copy.wait_send()
        for copy in wave_copies:
            copy.wait_recv()

    @pl.when(odd == 1)
    def _():
        lift_copy.wait_recv()
        for step in range(chunks):
            index = (step + chunks // 2) % chunks
            here = slice(index * group, (index + 1) * group)
            part[:, here] = first[:, here] + lift_in[:, here]
            part_copy(index).start()
        late_edges()
        relaxed(1, early_edges + 1)

        for index in range(chunks):
            here = slice(index * group, (index + 1) * group)
            part_copy((index + chunks // 2) % chunks).wait_recv()
            second[chip, :, here] = part[:, here] + part_in[:, here]
            second_copy(index).start()
        own_copy.start()
        pl.semaphore_signal(
            go_sem, inc=1, device_id=(sibling, sp), device_id_type=pl.DeviceIdType.MESH
        )

        def ascend(src, arriving, frame, dst, slot, sent, sends):
            for index in range(chunks):
                if index == 0:
                    arriving(0).wait_recv()
                if index + 1 < chunks:
                    arriving(index + 1).wait_recv()
                values = coarse_rows(src.at[0], frame, index * group + frame + 2)
                for field in range(3):
                    dst[slot, field, index * group : (index + 1) * group] = values[field] + take(
                        src.at[1, field], index * group + 2, group
                    )
                if sends is None:
                    sent(index).start()
                else:
                    @pl.when(sends)
                    def _():
                        sent(index).start()

        ascend(second, second_in, 0, third, pair, third_copy, None)
        relaxed(early_edges + 1, moments)
        ascend(third, third_in, 2, fourth, half, fourth_copy, inner)
        for index in range(chunks):
            fourth_in(index).wait_recv()

            @pl.when(inner)
            def _():
                fourth_in(index).start()

        coarse(fourth.at[0], 4, climb.at[0], 4, fourth.at[1], 4)
        coarse(climb.at[0], 4, climb.at[1], 4, climb.at[0], 4)

        def rise(bit, src, dst, added, added_frame):
            @pl.when(bit == 1)
            def _():
                coarse(src, 4, dst, 4, added, added_frame)

            @pl.when(bit == 0)
            def _():
                dst[...] = src[...]

        rise(half, climb.at[1], climb.at[0], fourth.at[0], 4)
        rise(pair, climb.at[0], climb.at[2], third.at[0], 2)
        rise(chip, climb.at[2], climb.at[1], second.at[0], 0)
        for copy in wave_copies:
            copy.start()
        here_copy.wait_recv()
        coarse(climb.at[1], 4, wave.at[0], 0, lower_here, 0)

        own_copy.wait_send()
        for index in range(chunks):
            part_copy(index).wait_send()
            second_copy(index).wait_send()
            third_copy(index).wait_send()

            @pl.when(inner)
            def _():
                fourth_copy(index).wait_send()
                fourth_in(index).wait_send()

        for copy in wave_copies:
            copy.wait_send()

    def store(src, dst, index):
        return [
            pltpu.make_async_copy(
                src.at[:, :, strip, :], dst.at[:, :, pl.ds(strip * lanes, lanes)],
                out_sems.at[index, strip],
            )
            for strip in range(strips)
        ]

    def store_moment(moment):
        return store(track.at[moment, :, 0:own], out.at[moment], moment)

    @pl.when(odd == 1)
    def _():
        own_in[...] = lower_here[:, 0:own]

    @pl.when(odd == 0)
    def _():
        own_in[...] = passed_in[...]

    own_in[0] = own_in[0] * (1.0 / height_scale)
    for copy in store(own_in, residual.at[0], moments):
        copy.start()

    def finish(moment, values):
        track[moment, 0, 0:own] = (1.0 / height_scale) * (values[0] + track[moment, 0, 0:own])
        track[moment, 1, 0:own] += values[1]
        track[moment, 2, 0:own] += values[2]
        for copy in store_moment(moment):
            copy.start()

    finish(0, wave[0, :, 0:own])

    def correct(moment, carry):
        a = (moment - 1) % 2
        b = moment % 2
        fine(wave.at[a], wave.at[b])
        finish(moment, wave[b, :, 0:own])
        return carry

    lax.fori_loop(1, moments, correct, 0)

    def drain(moment, carry):
        for copy in store_moment(moment):
            copy.wait()
        return carry

    lax.fori_loop(0, moments, drain, 0)
    for copy in store(own_in, residual.at[0], moments):
        copy.wait()


def kernel_body(cpoint_guess, tide_forcing, depth, drag):
    moments, fields, own, cols = tide_forcing.shape
    strips = cols // lanes
    rows = 2 * own
    chunks = rows // group

    def held(*shape):
        return pltpu.VMEM((*shape, strips, lanes), jnp.float32)

    dma = pltpu.SemaphoreType.DMA
    vmem = pl.BlockSpec(memory_space=pltpu.VMEM)
    return pl.pallas_call(
        cycle_kernel,
        out_shape=(
            jax.ShapeDtypeStruct(tide_forcing.shape, jnp.float32),
            jax.ShapeDtypeStruct(cpoint_guess.shape, jnp.float32),
        ),
        in_specs=[pl.BlockSpec(memory_space=pltpu.HBM)] * 4,
        out_specs=(vmem, vmem),
        scratch_shapes=[
            held(fields, own),
            held(moments, fields, own),
            held(2, own),
            held(2, own),
            held(rows),
            held(rows),
            held(rows),
            held(moments, fields, rows),
            held(fields, rows),
            held(moments - 1, 8),
            held(moments - 1, 8),
            held(fields, own),
            held(fields, own),
            held(fields, rows),
            held(fields, rows),
            held(fields, rows),
            held(fields, rows),
            held(fields, rows),
            held(2, fields, rows),
            held(2, fields, rows),
            held(2, fields, rows),
            held(3, fields, rows),
            held(2, fields, rows),
            held(fields, rows),
            held(fields, rows),
            held(fields, rows),
            held(fields, own),
            held(fields, own),
            held(fields, own),
            held(2, fields, own),
            held(fields, own),
            dma((5, strips)),
            dma((2,)),
            dma((2,)),
            dma((moments - 1,)),
            dma((moments - 1,)),
            dma((2,)),
            dma((chunks,)),
            dma((chunks,)),
            dma((chunks,)),
            dma((chunks,)),
            dma((chunks,)),
            dma((chunks,)),
            dma((chunks,)),
            dma((chunks,)),
            dma((chunks,)),
            dma((2,)),
            dma((2,)),
            dma((2,)),
            dma((2,)),
            dma((2,)),
            dma((3,)),
            dma((3,)),
            dma((moments + 1, strips)),
            pltpu.SemaphoreType.REGULAR,
        ],
        compiler_params=pltpu.CompilerParams(
            collective_id=0, has_side_effects=True, vmem_limit_bytes=61 * 1024 * 1024
        ),
    )(cpoint_guess, tide_forcing, depth, drag)


def solution(mesh):
    placed = (
        P("tm", None, "space", None),
        P("tm", None, "space", None),
        P("space", None),
        P("space", None),
    )
    one_top_point = mesh.shape["tm"] == 2 ** (LEVELS - 1)
    fits = one_top_point and mesh.shape["space"] == 2
    return jax.shard_map(
        kernel_body if fits else body,
        mesh=mesh,
        in_specs=placed,
        out_specs=(P("tm", None, "space", None), P("tm", None, "space", None)),
        check_vma=False,
    )
```

profile of v0, /device:TPU:0, one launch (start us, length us, event | category | flops | bytes accessed | tf_op | source)
XLA Modules:
  0.0 48.4 jit_solution(10932144134165273590)
XLA Ops:
  0.6 44.4 %shard_map.59 = (f32[8,3,16,1024]{3,2,1,0:T(8,128)}, f32[1,3,16,1024]{3,2,1,0:T(8,128)}) custom-call(f32[1,3,16,1024]{3,2,1,0:T(8,128)} %guess_hbm.1, f32[8,3,16,1024]{3,2,1,0:T(8,128)} %forcing_hbm.1, f32[16,1024]{1,0:T(8,128)} %depth_hbm.1, f32[16,1024]{1,0:T(8,128)} %drag_hbm.1), custom_call_target="tpu_custom_call" | custom-call | tf_op jit(solution)/shard_map/pallas_call | solution.py:590
  45.0 0.0 copy-start
  45.0 2.8 %copy.8 = f32[8,3,16,1024]{3,2,1,0:T(8,128)} copy(f32[8,3,16,1024]{3,2,1,0:T(8,128)} %get-tuple-element.4) | data formatting | bytes 3145728
  47.8 0.0 copy-done
  47.8 0.7 %copy.9 = f32[1,3,16,1024]{3,2,1,0:T(8,128)} copy(f32[1,3,16,1024]{3,2,1,0:T(8,128)S(1)} %copy-done) | data formatting | bytes 393216
Async XLA Ops:
  45.0 2.8 %copy-start = (f32[1,3,16,1024]{3,2,1,0:T(8,128)S(1)}, f32[1,3,16,1024]{3,2,1,0:T(8,128)}, u32[]{:S(2)}) copy-start(f32[1,3,16,1024]{3,2,1,0:T(8,128)} %get-tuple-element.5) | copy-start | bytes 589828
where the time goes:
time: 48.6 us; the launch traced here: 48.4 us
  Pallas kernels  44.4 us (91%)
  local copies, waits for them, and re-layouts  3.45 us (7%)
  between operations  0.65 us (1%)
    pallas_call x1, Pallas kernels, kernel_body(): pl.pallas_call(cycle_kernel, out_shape=(jax.ShapeDtypeStruct(tide_forcing...  44.4 us
    unnamed x4, local copies, waits for them, and re-layouts  3.45 us

commit v1 on v0

--- a/solution.py
+++ b/solution.py
@@ -125,14 +125,66 @@
 early_edges = 3
 
 
+def down_cols(a):
+    here = lax.broadcasted_iota(jnp.int32, a.shape, 2)
+    following = jnp.where(here == 0, pltpu.roll(a, a.shape[1] - 1, 1), a)
+    preceding = jnp.where(here == lanes - 1, pltpu.roll(a, 1, 1), a)
+    return pltpu.roll(following, lanes - 1, 2) - pltpu.roll(preceding, 1, 2)
+
+
+def take(ref, start, size):
+    total = ref.shape[0]
+    start %= total
+    if start + size <= total:
+        return ref[start : start + size]
+    return jnp.concatenate([ref[start:total], ref[0 : start + size - total]], axis=0)
+
+
+def raise_heights(h, u_before, u_after, v, depths):
+    return h - depths * (u_after - u_before + down_cols(v))
+
+
+def new_speeds(u, v, h_before, h, h_after, kept, courant):
+    turn = courant * coriolis
+    east = h_after - h_before
+    north = down_cols(h)
+    slope = courant * 0.5 / height_scale
+    if slope != 1.0:
+        east = slope * east
+        north = slope * north
+    return kept * u + turn * v - east, kept * v - turn * u - north
+
+
+def fine_substep(src, dst, depths, kept):
+    rows = src.shape[1]
+    for r in range(0, rows, group):
+        dst[0, r : r + group] = raise_heights(
+            src[0, r : r + group], take(src.at[1], r - 1, group), take(src.at[1], r + 1, group),
+            src[2, r : r + group], depths[r : r + group],
+        )
+    for r in range(0, rows, group):
+        east, north = new_speeds(
+            src[1, r : r + group], src[2, r : r + group], take(dst.at[0], r - 1, group),
+            dst[0, r : r + group], take(dst.at[0], r + 1, group), kept[r : r + group],
+            fine_courant,
+        )
+        dst[1, r : r + group] = east
+        dst[2, r : r + group] = north
+
+
+def fine_step(src, middle, dst, depths, kept):
+    fine_substep(src, middle, depths, kept)
+    fine_substep(middle, dst, depths, kept)
+
+
 def cycle_kernel(
-    guess_hbm, forcing_hbm, depth_hbm, drag_hbm, out, residual,
-    guess, forcing, raw, raw_in, fine_depth, coarse_depth, retain, track, mid, edges, edges_in,
+    guess_hbm, forcing_hbm, depth_hbm, drag_hbm, track, corrected, own_part, fine_depth, retain,
+    guess, forcing, raw, raw_in, coarse_depth, mid, edges, edges_in,
     ahead, ahead_in, first, lift, lift_in, part, part_in, second, third, fourth, climb, wave,
     lower_in, lower, lower_here, own_in, passed, passed_in, relax, relax_mid,
     load_sems, coef_sems, ahead_sems, edge_send, edge_recv, lift_sems, part_send, part_recv,
     second_send, second_recv, third_send, third_recv, fourth_send, fourth_recv, relay_send,
-    lower_send, lower_recv, here_sems, own_sems, passed_sems, wave_send, wave_recv, out_sems, go_sem,
+    lower_send, lower_recv, here_sems, own_sems, passed_sems, wave_send, wave_recv, go_sem,
 ):
     tm = lax.axis_index("tm")
     sp = lax.axis_index("space")
@@ -190,52 +242,8 @@
         for copy in copies:
             copy.start()
 
-    lane = lax.broadcasted_iota(jnp.int32, (1, strips, lanes), 2)
-
-    def down_cols(a):
-        here = lax.broadcasted_iota(jnp.int32, a.shape, 2)
-        following = jnp.where(here == 0, pltpu.roll(a, strips - 1, 1), a)
-        preceding = jnp.where(here == lanes - 1, pltpu.roll(a, 1, 1), a)
-        return pltpu.roll(following, lanes - 1, 2) - pltpu.roll(preceding, 1, 2)
-
-    def take(ref, start, size):
-        total = ref.shape[0]
-        start %= total
-        if start + size <= total:
-            return ref[start : start + size]
-        return jnp.concatenate([ref[start:total], ref[0 : start + size - total]], axis=0)
-
-    def raise_heights(h, u_before, u_after, v, depths):
-        return h - depths * (u_after - u_before + down_cols(v))
-
-    def new_speeds(u, v, h_before, h, h_after, kept, courant):
-        turn = courant * coriolis
-        east = h_after - h_before
-        north = down_cols(h)
-        slope = courant * 0.5 / height_scale
-        if slope != 1.0:
-            east = slope * east
-            north = slope * north
-        return kept * u + turn * v - east, kept * v - turn * u - north
-
-    def fine_substep(src, dst):
-        for r in range(0, rows, group):
-            dst[0, r : r + group] = raise_heights(
-                src[0, r : r + group], take(src.at[1], r - 1, group), take(src.at[1], r + 1, group),
-                src[2, r : r + group], fine_depth[r : r + group],
-            )
-        for r in range(0, rows, group):
-            east, north = new_speeds(
-                src[1, r : r + group], src[2, r : r + group], take(dst.at[0], r - 1, group),
-                dst[0, r : r + group], take(dst.at[0], r + 1, group), retain[r : r + group],
-                fine_courant,
-            )
-            dst[1, r : r + group] = east
-            dst[2, r : r + group] = north
-
     def fine(src, dst):
-        fine_substep(src, mid)
-        fine_substep(mid, dst)
+        fine_step(src, mid, dst, fine_depth, retain)
 
     def coarse_rows(src, frame, row, size=group):
         start = row - frame
@@ -251,13 +259,30 @@
         return h[1 : size + 1], east, north
 
     def coarse(src, frame, dst, dst_frame, added=None, added_frame=0):
+        def plus(value, field, row):
+            if added is None:
+                return value
+            return value + take(added.at[field], row - added_frame, group)
+
         for r in range(0, rows, group):
-            values = coarse_rows(src, frame, r + dst_frame)
-            for field in range(3):
-                value = values[field]
-                if added is not None:
-                    value = value + take(added.at[field], r + dst_frame - added_frame, group)
-                dst[field, r : r + group] = value
+            row = r + dst_frame
+            start = row - frame
+            mid[0, r : r + group] = raise_heights(
+                take(src.at[0], start, group), take(src.at[1], start - 1, group),
+                take(src.at[1], start + 1, group), take(src.at[2], start, group),
+                take(coarse_depth, row, group),
+            )
+        for r in range(0, rows, group):
+            row = r + dst_frame
+            start = row - frame
+            here = mid[0, r : r + group]
+            east, north = new_speeds(
+                take(src.at[1], start, group), take(src.at[2], start, group),
+                take(mid.at[0], r - 1, group), here, take(mid.at[0], r + 1, group),
+                take(retain, row, group), coarse_courant,
+            )
+            for field, value in enumerate((here, east, north)):
+                dst[field, r : r + group] = plus(value, field, row)
 
     for copies in loads[:2]:
         for copy in copies:
@@ -524,6 +549,22 @@
         for copy in wave_copies:
             copy.wait_send()
 
+    corrected[...] = wave[0]
+
+    @pl.when(odd == 1)
+    def _():
+        own_part[...] = lower_here[:, 0:own]
+
+    @pl.when(odd == 0)
+    def _():
+        own_part[...] = passed_in[...]
+
+
+def finish_kernel(
+    track, corrected, own_part, fine_depth, retain, out, residual, wave, mid, ready, ready_part, out_sems
+):
+    moments, _, own, strips, _ = ready.shape
+
     def store(src, dst, index):
         return [
             pltpu.make_async_copy(
@@ -533,46 +574,37 @@
             for strip in range(strips)
         ]
 
-    def store_moment(moment):
-        return store(track.at[moment, :, 0:own], out.at[moment], moment)
-
-    @pl.when(odd == 1)
-    def _():
-        own_in[...] = lower_here[:, 0:own]
-
-    @pl.when(odd == 0)
-    def _():
-        own_in[...] = passed_in[...]
-
-    own_in[0] = own_in[0] * (1.0 / height_scale)
-    for copy in store(own_in, residual.at[0], moments):
+    ready_part[0] = own_part[0] * (1.0 / height_scale)
+    ready_part[1:3] = own_part[1:3]
+    for copy in store(ready_part, residual.at[0], moments):
         copy.start()
 
     def finish(moment, values):
-        track[moment, 0, 0:own] = (1.0 / height_scale) * (values[0] + track[moment, 0, 0:own])
-        track[moment, 1, 0:own] += values[1]
-        track[moment, 2, 0:own] += values[2]
-        for copy in store_moment(moment):
+        ready[moment, 0] = (1.0 / height_scale) * (values[0] + track[moment, 0, 0:own])
+        ready[moment, 1] = values[1] + track[moment, 1, 0:own]
+        ready[moment, 2] = values[2] + track[moment, 2, 0:own]
+        for copy in store(ready.at[moment], out.at[moment], moment):
             copy.start()
 
-    finish(0, wave[0, :, 0:own])
+    wave[0] = corrected[...]
+    finish(0, corrected[:, 0:own])
 
     def correct(moment, carry):
         a = (moment - 1) % 2
         b = moment % 2
-        fine(wave.at[a], wave.at[b])
+        fine_step(wave.at[a], mid, wave.at[b], fine_depth, retain)
         finish(moment, wave[b, :, 0:own])
         return carry
 
     lax.fori_loop(1, moments, correct, 0)
 
     def drain(moment, carry):
-        for copy in store_moment(moment):
+        for copy in store(ready.at[moment], out.at[moment], moment):
             copy.wait()
         return carry
 
     lax.fori_loop(0, moments, drain, 0)
-    for copy in store(own_in, residual.at[0], moments):
+    for copy in store(ready_part, residual.at[0], moments):
         copy.wait()
 
 
@@ -587,23 +619,27 @@
 
     dma = pltpu.SemaphoreType.DMA
     vmem = pl.BlockSpec(memory_space=pltpu.VMEM)
-    return pl.pallas_call(
+    def given(*shape):
+        return jax.ShapeDtypeStruct((*shape, strips, lanes), jnp.float32)
+
+    hbm = pl.BlockSpec(memory_space=pltpu.HBM)
+    passed_on = pl.pallas_call(
         cycle_kernel,
         out_shape=(
-            jax.ShapeDtypeStruct(tide_forcing.shape, jnp.float32),
-            jax.ShapeDtypeStruct(cpoint_guess.shape, jnp.float32),
+            given(moments, fields, rows),
+            given(fields, rows),
+            given(fields, own),
+            given(rows),
+            given(rows),
         ),
-        in_specs=[pl.BlockSpec(memory_space=pltpu.HBM)] * 4,
-        out_specs=(vmem, vmem),
+        in_specs=[hbm] * 4,
+        out_specs=(vmem,) * 5,
         scratch_shapes=[
             held(fields, own),
             held(moments, fields, own),
             held(2, own),
             held(2, own),
             held(rows),
-            held(rows),
-            held(rows),
-            held(moments, fields, rows),
             held(fields, rows),
             held(moments - 1, 8),
             held(moments - 1, 8),
@@ -649,13 +685,32 @@
             dma((2,)),
             dma((3,)),
             dma((3,)),
-            dma((moments + 1, strips)),
             pltpu.SemaphoreType.REGULAR,
         ],
         compiler_params=pltpu.CompilerParams(
-            collective_id=0, has_side_effects=True, vmem_limit_bytes=61 * 1024 * 1024
+            collective_id=0, has_side_effects=True, vmem_limit_bytes=32 * 1024 * 1024
         ),
-    )(cpoint_guess, tide_forcing, depth, drag)
+    )(*(
+        pltpu.with_memory_space_constraint(array, pltpu.HBM)
+        for array in (cpoint_guess, tide_forcing, depth, drag)
+    ))
+    return pl.pallas_call(
+        finish_kernel,
+        out_shape=(
+            jax.ShapeDtypeStruct(tide_forcing.shape, jnp.float32),
+            jax.ShapeDtypeStruct(cpoint_guess.shape, jnp.float32),
+        ),
+        in_specs=[vmem] * 5,
+        out_specs=(hbm, hbm),
+        scratch_shapes=[
+            held(2, fields, rows),
+            held(fields, rows),
+            held(moments, fields, own),
+            held(fields, own),
+            dma((moments + 1, strips)),
+        ],
+        compiler_params=pltpu.CompilerParams(vmem_limit_bytes=16 * 1024 * 1024),
+    )(*passed_on)
 
 
 def solution(mesh):

time: 48.6 us -> 42.7 us (0.88)
  local copies, waits for them, and re-layouts: 3.45 us -> 0 us
  Pallas kernels: 44.4 us -> 41.9 us
    unnamed x4 -> x0, local copies, waits for them, and re-layouts: 3.45 us -> none
    pallas_call x1 -> x2, Pallas kernels: 44.4 us -> 41.9 us  [the longest x1 37.6 us: kernel_body(): pl.pallas_call(cycle_kernel, out_shape=(given(moments, fields, rows), giv...]
where the time goes in v1:
time: 42.7 us; the launch traced here: 42.5 us
  Pallas kernels  41.9 us (98%)
  between operations  0.64 us (1%)
    pallas_call x1, Pallas kernels, kernel_body(): pl.pallas_call(cycle_kernel, out_shape=(given(moments, fields, rows), giv...  37.6 us
    pallas_call x1, Pallas kernels, kernel_body(): pl.pallas_call(finish_kernel, out_shape=(jax.ShapeDtypeStruct(tide_forcin...  4.32 us

profile of v1, /device:TPU:0, one launch (start us, length us, event | category | flops | bytes accessed | tf_op | source)
XLA Modules:
  0.0 42.5 jit_solution(17879552488045008732)
XLA Ops:
  0.6 37.6 %shard_map.59 = (f32[8,3,32,8,128]{4,3,2,1,0:T(8,128)S(1)}, f32[3,32,8,128]{3,2,1,0:T(8,128)S(1)}, f32[3,16,8,128]{3,2,1,0:T(8,128)S(1)}, f32[32,8,128]{2,1,0:T(8,128)S(1)}, f32[32,8,128]{2,1,0:T(8,128)S(1)}) custom-call(f32[1,3,16,1024]{3,2,1,0:T(8,128)} %guess_hbm.1, f32[8,3,16,1024]{3,2,1,0:T(8,128)} %forcing_hbm.1, f32[16,1024]{1,0:T(8,128)} %depth_hbm.1, ...), custom_call_target="tpu_custom_call" | custom-call | tf_op jit(solution)/shard_map/pallas_call | solution.py:626
  38.2 4.3 %shard_map.60 = (f32[8,3,16,1024]{3,2,1,0:T(8,128)}, f32[1,3,16,1024]{3,2,1,0:T(8,128)}) custom-call(f32[8,3,32,8,128]{4,3,2,1,0:T(8,128)S(1)} %get-tuple-element.7.track, f32[3,32,8,128]{3,2,1,0:T(8,128)S(1)} %get-tuple-element.8.corrected, f32[3,16,8,128]{3,2,1,0:T(8,128)S(1)} %get-tuple-element.9.own_part, ...), custom_call_target="tpu_custom_call" | custom-call | tf_op jit(solution)/shard_map/pallas_call | solution.py:697

commit v2 on v1

--- a/solution.py
+++ b/solution.py
@@ -121,6 +121,8 @@
 
 lanes = 128
 group = 4
+piece = 2
+lift_piece = 8
 height_scale = 0.125
 early_edges = 3
 
@@ -182,7 +184,7 @@
     guess, forcing, raw, raw_in, coarse_depth, mid, edges, edges_in,
     ahead, ahead_in, first, lift, lift_in, part, part_in, second, third, fourth, climb, wave,
     lower_in, lower, lower_here, own_in, passed, passed_in, relax, relax_mid,
-    load_sems, coef_sems, ahead_sems, edge_send, edge_recv, lift_sems, part_send, part_recv,
+    load_sems, coef_sems, ahead_sems, edge_send, edge_recv, lift_send, lift_recv, part_send, part_recv,
     second_send, second_recv, third_send, third_recv, fourth_send, fourth_recv, relay_send,
     lower_send, lower_recv, here_sems, own_sems, passed_sems, wave_send, wave_recv, go_sem,
 ):
@@ -193,7 +195,7 @@
     own = guess.shape[1]
     rows = 2 * own
     strips = guess.shape[2]
-    chunks = rows // group
+    chunks = rows // piece
     other = 1 - sp
     odd = tm % 2
     chip = (tm // 2) % 2
@@ -238,7 +240,7 @@
         partners.append(((tm + count - distance) % count, sp))
     for to in partners:
         pl.semaphore_signal(barrier, inc=1, device_id=to, device_id_type=pl.DeviceIdType.MESH)
-    for copies in loads:
+    for copies in loads[:2]:
         for copy in copies:
             copy.start()
 
@@ -288,8 +290,22 @@
         for copy in copies:
             copy.wait()
     pl.semaphore_wait(barrier, len(partners))
-    coef_copy = remote(raw, raw_in, coef_sems.at[0], coef_sems.at[1], (tm, other))
+    middle = own // 2
+    mine = pl.ds(odd * middle, middle)
+    theirs = pl.ds((1 - odd) * middle, middle)
+    coef_copy = remote(
+        raw.at[:, mine], raw_in.at[:, mine], coef_sems.at[0], coef_sems.at[1], (tm, other)
+    )
+    coef_share = remote(
+        raw_in.at[:, mine], raw_in.at[:, mine], coef_sems.at[2], coef_sems.at[3], (sibling, sp)
+    )
+    coef_shared = remote(
+        raw_in.at[:, theirs], raw_in.at[:, theirs], coef_sems.at[2], coef_sems.at[3], (sibling, sp)
+    )
     coef_copy.start()
+    for copies in loads[2:]:
+        for copy in copies:
+            copy.start()
 
     for copies in loads[2:4]:
         for copy in copies:
@@ -309,9 +325,13 @@
     fine_depth[0:own] = (fine_courant * 0.5 * height_scale) * raw[0]
     coarse_depth[0:own] = (coarse_courant * 0.5 * height_scale) * raw[0]
     retain[0:own] = 1.0 - raw[1]
+    coef_copy.wait_recv()
+    coef_share.start()
     for copy in loads[4]:
         copy.wait()
-    coef_copy.wait()
+    coef_copy.wait_send()
+    coef_shared.wait_recv()
+    coef_share.wait_send()
     fine_depth[own:rows] = (fine_courant * 0.5 * height_scale) * raw_in[0]
     coarse_depth[own:rows] = (coarse_courant * 0.5 * height_scale) * raw_in[0]
     retain[own:rows] = 1.0 - raw_in[1]
@@ -393,9 +413,18 @@
         lax.fori_loop(early_edges, moments - 1, step, 0)
 
     def span(index):
-        return pl.ds(index * group, group)
-
-    lift_copy = remote(lift, lift_in, lift_sems.at[0], lift_sems.at[1], (sibling, sp))
+        return pl.ds(index * piece, piece)
+
+    lift_pieces = rows // lift_piece
+    lift_order = [(index + lift_pieces // 2) % lift_pieces for index in range(lift_pieces)]
+
+    def lift_copy(index):
+        here = pl.ds(index * lift_piece, lift_piece)
+        return remote(
+            lift.at[:, here], lift_in.at[:, here], lift_send.at[index], lift_recv.at[index],
+            (sibling, sp),
+        )
+
     here_copy = remote(lower, lower_here, here_sems.at[0], here_sems.at[1], (sibling, sp))
     own_copy = remote(
         second.at[chip, :, 0:own], own_in, own_sems.at[0], own_sems.at[1], (sibling, sp)
@@ -409,12 +438,13 @@
         for index, start in enumerate((0, own))
     ]
     top_frame = 4
+    wave_pieces = ((0, own), (own, rows - top_frame), (rows - top_frame, rows))
     wave_copies = [
         remote(
             climb.at[1, :, start:end], wave.at[0, :, (start + top_frame) % rows : (end + top_frame - 1) % rows + 1],
             wave_send.at[index], wave_recv.at[index], (sibling, sp),
         )
-        for index, (start, end) in enumerate(((0, own), (own, rows - top_frame), (rows - top_frame, rows)))
+        for index, (start, end) in enumerate(wave_pieces)
     ]
 
     def part_copy(index):
@@ -442,14 +472,17 @@
 
     @pl.when(odd == 0)
     def _():
-        coarse(first, 0, lift, 0)
-        lift_copy.start()
+        for index in lift_order:
+            start = index * lift_piece
+            values = coarse_rows(first, 0, start, lift_piece)
+            for field in range(3):
+                lift[field, start : start + lift_piece] = values[field]
+            lift_copy(index).start()
         relaxed(1, early_edges + 1)
         pl.semaphore_wait(go_sem, 1)
-        late_edges()
         for copy in lower_copies:
             copy.start()
-        relaxed(early_edges + 1, moments)
+        late_edges()
         own_copy.wait_recv()
         for copy in lower_copies:
             copy.wait()
@@ -460,7 +493,9 @@
             for field in range(3):
                 passed[field, r : r + group] = own_in[field, r : r + group] - values[field]
         passed_copy.start()
-        lift_copy.wait_send()
+        relaxed(early_edges + 1, moments)
+        for index in lift_order:
+            lift_copy(index).wait_send()
         passed_copy.wait()
         here_copy.wait_send()
         for copy in wave_copies:
@@ -468,35 +503,39 @@
 
     @pl.when(odd == 1)
     def _():
-        lift_copy.wait_recv()
-        for step in range(chunks):
-            index = (step + chunks // 2) % chunks
-            here = slice(index * group, (index + 1) * group)
-            part[:, here] = first[:, here] + lift_in[:, here]
-            part_copy(index).start()
+        for index in lift_order:
+            lift_copy(index).wait_recv()
+            for inside in range(lift_piece // piece):
+                chunk = index * (lift_piece // piece) + inside
+                here = slice(chunk * piece, (chunk + 1) * piece)
+                part[:, here] = first[:, here] + lift_in[:, here]
+                part_copy(chunk).start()
         late_edges()
         relaxed(1, early_edges + 1)
 
         for index in range(chunks):
-            here = slice(index * group, (index + 1) * group)
+            here = slice(index * piece, (index + 1) * piece)
             part_copy((index + chunks // 2) % chunks).wait_recv()
             second[chip, :, here] = part[:, here] + part_in[:, here]
             second_copy(index).start()
+            if index == chunks // 2:
+                pl.semaphore_signal(
+                    go_sem, inc=1, device_id=(sibling, sp), device_id_type=pl.DeviceIdType.MESH
+                )
+
         own_copy.start()
-        pl.semaphore_signal(
-            go_sem, inc=1, device_id=(sibling, sp), device_id_type=pl.DeviceIdType.MESH
-        )
 
         def ascend(src, arriving, frame, dst, slot, sent, sends):
             for index in range(chunks):
                 if index == 0:
                     arriving(0).wait_recv()
-                if index + 1 < chunks:
-                    arriving(index + 1).wait_recv()
-                values = coarse_rows(src.at[0], frame, index * group + frame + 2)
+                    arriving(1).wait_recv()
+                if index + 2 < chunks:
+                    arriving(index + 2).wait_recv()
+                values = coarse_rows(src.at[0], frame, index * piece + frame + 2, piece)
                 for field in range(3):
-                    dst[slot, field, index * group : (index + 1) * group] = values[field] + take(
-                        src.at[1, field], index * group + 2, group
+                    dst[slot, field, index * piece : (index + 1) * piece] = values[field] + take(
+                        src.at[1, field], index * piece + 2, piece
                     )
                 if sends is None:
                     sent(index).start()
@@ -529,8 +568,20 @@
 
         rise(half, climb.at[1], climb.at[0], fourth.at[0], 4)
         rise(pair, climb.at[0], climb.at[2], third.at[0], 2)
-        rise(chip, climb.at[2], climb.at[1], second.at[0], 0)
-        for copy in wave_copies:
+
+        for (start, end), copy in zip(wave_pieces, wave_copies):
+            @pl.when(chip == 1)
+            def _():
+                values = coarse_rows(climb.at[2], 4, start + 4, end - start)
+                for field in range(3):
+                    climb[1, field, start:end] = values[field] + take(
+                        second.at[0, field], start + 4, end - start
+                    )
+
+            @pl.when(chip == 0)
+            def _():
+                climb[1, :, start:end] = climb[2, :, start:end]
+
             copy.start()
         here_copy.wait_recv()
         coarse(climb.at[1], 4, wave.at[0], 0, lower_here, 0)
@@ -574,32 +625,39 @@
             for strip in range(strips)
         ]
 
+    def ready_copies(moment):
+        return store(ready.at[moment], out.at[moment], moment)
+
+    def finish(moment, values):
+        ready[moment, 0] = (1.0 / height_scale) * (values[0] + track[moment, 0, 0:own])
+        ready[moment, 1] = values[1] + track[moment, 1, 0:own]
+        ready[moment, 2] = values[2] + track[moment, 2, 0:own]
+
+    finish(0, corrected[:, 0:own])
     ready_part[0] = own_part[0] * (1.0 / height_scale)
     ready_part[1:3] = own_part[1:3]
     for copy in store(ready_part, residual.at[0], moments):
         copy.start()
-
-    def finish(moment, values):
-        ready[moment, 0] = (1.0 / height_scale) * (values[0] + track[moment, 0, 0:own])
-        ready[moment, 1] = values[1] + track[moment, 1, 0:own]
-        ready[moment, 2] = values[2] + track[moment, 2, 0:own]
-        for copy in store(ready.at[moment], out.at[moment], moment):
-            copy.start()
-
-    wave[0] = corrected[...]
-    finish(0, corrected[:, 0:own])
+    fine_step(corrected, mid, wave.at[1], fine_depth, retain)
+    finish(1, wave[1, :, 0:own])
+    for copy in ready_copies(0):
+        copy.start()
 
     def correct(moment, carry):
         a = (moment - 1) % 2
         b = moment % 2
+        for copy in ready_copies(moment - 1):
+            copy.start()
         fine_step(wave.at[a], mid, wave.at[b], fine_depth, retain)
         finish(moment, wave[b, :, 0:own])
         return carry
 
-    lax.fori_loop(1, moments, correct, 0)
+    lax.fori_loop(2, moments, correct, 0)
+    for copy in ready_copies(moments - 1):
+        copy.start()
 
     def drain(moment, carry):
-        for copy in store(ready.at[moment], out.at[moment], moment):
+        for copy in ready_copies(moment):
             copy.wait()
         return carry
 
@@ -612,7 +670,7 @@
     moments, fields, own, cols = tide_forcing.shape
     strips = cols // lanes
     rows = 2 * own
-    chunks = rows // group
+    chunks = rows // piece
 
     def held(*shape):
         return pltpu.VMEM((*shape, strips, lanes), jnp.float32)
@@ -664,11 +722,12 @@
             held(2, fields, own),
             held(fields, own),
             dma((5, strips)),
-            dma((2,)),
+            dma((4,)),
             dma((2,)),
             dma((moments - 1,)),
             dma((moments - 1,)),
-            dma((2,)),
+            dma((rows // lift_piece,)),
+            dma((rows // lift_piece,)),
             dma((chunks,)),
             dma((chunks,)),
             dma((chunks,)),

time: 42.7 us -> 42.8 us (level)
  no operation moved by 1% of the time
where the time goes in v2:
time: 42.8 us; the launch traced here: 42.4 us
  Pallas kernels  41.7 us (97%)
  between operations  0.64 us (1%)
    pallas_call x1, Pallas kernels, kernel_body(): pl.pallas_call(cycle_kernel, out_shape=(given(moments, fields, rows), giv...  37.2 us
    pallas_call x1, Pallas kernels, kernel_body(): pl.pallas_call(finish_kernel, out_shape=(jax.ShapeDtypeStruct(tide_forcin...  4.48 us

profile of v2, /device:TPU:0, one launch (start us, length us, event | category | flops | bytes accessed | tf_op | source)
XLA Modules:
  0.0 42.4 jit_solution(457705107089828648)
XLA Ops:
  0.6 37.2 %shard_map.59 = (f32[8,3,32,8,128]{4,3,2,1,0:T(8,128)S(1)}, f32[3,32,8,128]{3,2,1,0:T(8,128)S(1)}, f32[3,16,8,128]{3,2,1,0:T(8,128)S(1)}, f32[32,8,128]{2,1,0:T(8,128)S(1)}, f32[32,8,128]{2,1,0:T(8,128)S(1)}) custom-call(f32[1,3,16,1024]{3,2,1,0:T(8,128)} %guess_hbm.1, f32[8,3,16,1024]{3,2,1,0:T(8,128)} %forcing_hbm.1, f32[16,1024]{1,0:T(8,128)} %depth_hbm.1, ...), custom_call_target="tpu_custom_call" | custom-call | tf_op jit(solution)/shard_map/pallas_call | solution.py:684
  37.9 4.5 %shard_map.60 = (f32[8,3,16,1024]{3,2,1,0:T(8,128)}, f32[1,3,16,1024]{3,2,1,0:T(8,128)}) custom-call(f32[8,3,32,8,128]{4,3,2,1,0:T(8,128)S(1)} %get-tuple-element.7.track, f32[3,32,8,128]{3,2,1,0:T(8,128)S(1)} %get-tuple-element.8.corrected, f32[3,16,8,128]{3,2,1,0:T(8,128)S(1)} %get-tuple-element.9.own_part, ...), custom_call_target="tpu_custom_call" | custom-call | tf_op jit(solution)/shard_map/pallas_call | solution.py:756

commit v3 on v2

--- a/solution.py
+++ b/solution.py
@@ -545,14 +545,22 @@
                         sent(index).start()
 
         ascend(second, second_in, 0, third, pair, third_copy, None)
-        relaxed(early_edges + 1, moments)
         ascend(third, third_in, 2, fourth, half, fourth_copy, inner)
+
+        @pl.when(jnp.logical_not(inner))
+        def _():
+            relaxed(early_edges + 1, moments)
+
         for index in range(chunks):
             fourth_in(index).wait_recv()
 
             @pl.when(inner)
             def _():
                 fourth_in(index).start()
+
+        @pl.when(inner)
+        def _():
+            relaxed(early_edges + 1, moments)
 
         coarse(fourth.at[0], 4, climb.at[0], 4, fourth.at[1], 4)
         coarse(climb.at[0], 4, climb.at[1], 4, climb.at[0], 4)
@@ -625,39 +633,32 @@
             for strip in range(strips)
         ]
 
-    def ready_copies(moment):
-        return store(ready.at[moment], out.at[moment], moment)
+    ready_part[0] = own_part[0] * (1.0 / height_scale)
+    ready_part[1:3] = own_part[1:3]
+    for copy in store(ready_part, residual.at[0], moments):
+        copy.start()
 
     def finish(moment, values):
         ready[moment, 0] = (1.0 / height_scale) * (values[0] + track[moment, 0, 0:own])
         ready[moment, 1] = values[1] + track[moment, 1, 0:own]
         ready[moment, 2] = values[2] + track[moment, 2, 0:own]
-
+        for copy in store(ready.at[moment], out.at[moment], moment):
+            copy.start()
+
+    wave[0] = corrected[...]
     finish(0, corrected[:, 0:own])
-    ready_part[0] = own_part[0] * (1.0 / height_scale)
-    ready_part[1:3] = own_part[1:3]
-    for copy in store(ready_part, residual.at[0], moments):
-        copy.start()
-    fine_step(corrected, mid, wave.at[1], fine_depth, retain)
-    finish(1, wave[1, :, 0:own])
-    for copy in ready_copies(0):
-        copy.start()
 
     def correct(moment, carry):
         a = (moment - 1) % 2
         b = moment % 2
-        for copy in ready_copies(moment - 1):
-            copy.start()
         fine_step(wave.at[a], mid, wave.at[b], fine_depth, retain)
         finish(moment, wave[b, :, 0:own])
         return carry
 
-    lax.fori_loop(2, moments, correct, 0)
-    for copy in ready_copies(moments - 1):
-        copy.start()
+    lax.fori_loop(1, moments, correct, 0)
 
     def drain(moment, carry):
-        for copy in ready_copies(moment):
+        for copy in store(ready.at[moment], out.at[moment], moment):
             copy.wait()
         return carry
 

time: 42.8 us -> 42.6 us (level)
  no operation moved by 1% of the time
where the time goes in v3:
time: 42.6 us; the launch traced here: 42.2 us
  Pallas kernels  41.6 us (98%)
  between operations  0.64 us (2%)
    pallas_call x1, Pallas kernels, kernel_body(): pl.pallas_call(cycle_kernel, out_shape=(given(moments, fields, rows), giv...  37.2 us
    pallas_call x1, Pallas kernels, kernel_body(): pl.pallas_call(finish_kernel, out_shape=(jax.ShapeDtypeStruct(tide_forcin...  4.32 us

profile of v3, /device:TPU:0, one launch (start us, length us, event | category | flops | bytes accessed | tf_op | source)
XLA Modules:
  0.0 42.2 jit_solution(11359819299015461418)
XLA Ops:
  0.6 37.2 %shard_map.59 = (f32[8,3,32,8,128]{4,3,2,1,0:T(8,128)S(1)}, f32[3,32,8,128]{3,2,1,0:T(8,128)S(1)}, f32[3,16,8,128]{3,2,1,0:T(8,128)S(1)}, f32[32,8,128]{2,1,0:T(8,128)S(1)}, f32[32,8,128]{2,1,0:T(8,128)S(1)}) custom-call(f32[1,3,16,1024]{3,2,1,0:T(8,128)} %guess_hbm.1, f32[8,3,16,1024]{3,2,1,0:T(8,128)} %forcing_hbm.1, f32[16,1024]{1,0:T(8,128)} %depth_hbm.1, ...), custom_call_target="tpu_custom_call" | custom-call | tf_op jit(solution)/shard_map/pallas_call | solution.py:685
  37.9 4.3 %shard_map.60 = (f32[8,3,16,1024]{3,2,1,0:T(8,128)}, f32[1,3,16,1024]{3,2,1,0:T(8,128)}) custom-call(f32[8,3,32,8,128]{4,3,2,1,0:T(8,128)S(1)} %get-tuple-element.7.track, f32[3,32,8,128]{3,2,1,0:T(8,128)S(1)} %get-tuple-element.8.corrected, f32[3,16,8,128]{3,2,1,0:T(8,128)S(1)} %get-tuple-element.9.own_part, ...), custom_call_target="tpu_custom_call" | custom-call | tf_op jit(solution)/shard_map/pallas_call | solution.py:757

commit v4 on v3

--- a/solution.py
+++ b/solution.py
@@ -121,8 +121,9 @@
 
 lanes = 128
 group = 4
-piece = 2
+piece = 4
 lift_piece = 8
+ahead_pieces = 4 // piece
 height_scale = 0.125
 early_edges = 3
 
@@ -529,9 +530,10 @@
             for index in range(chunks):
                 if index == 0:
                     arriving(0).wait_recv()
-                    arriving(1).wait_recv()
-                if index + 2 < chunks:
-                    arriving(index + 2).wait_recv()
+                    if piece < 4:
+                        arriving(1).wait_recv()
+                if index + ahead_pieces < chunks:
+                    arriving(index + ahead_pieces).wait_recv()
                 values = coarse_rows(src.at[0], frame, index * piece + frame + 2, piece)
                 for field in range(3):
                     dst[slot, field, index * piece : (index + 1) * piece] = values[field] + take(

time: 42.6 us -> 41.8 us (0.981)
  Pallas kernels: 41.6 us -> 40.8 us
    pallas_call x1, Pallas kernels: 37.2 us -> 36.5 us  [kernel_body(): pl.pallas_call(cycle_kernel, out_shape=(given(moments, fields, rows), giv...]
where the time goes in v4:
time: 41.8 us; the launch traced here: 41.4 us
  Pallas kernels  40.8 us (98%)
  between operations  0.64 us (2%)
    pallas_call x1, Pallas kernels, kernel_body(): pl.pallas_call(cycle_kernel, out_shape=(given(moments, fields, rows), giv...  36.5 us
    pallas_call x1, Pallas kernels, kernel_body(): pl.pallas_call(finish_kernel, out_shape=(jax.ShapeDtypeStruct(tide_forcin...  4.32 us

profile of v4, /device:TPU:0, one launch (start us, length us, event | category | flops | bytes accessed | tf_op | source)
XLA Modules:
  0.0 41.4 jit_solution(17950005786911876051)
XLA Ops:
  0.6 36.5 %shard_map.59 = (f32[8,3,32,8,128]{4,3,2,1,0:T(8,128)S(1)}, f32[3,32,8,128]{3,2,1,0:T(8,128)S(1)}, f32[3,16,8,128]{3,2,1,0:T(8,128)S(1)}, f32[32,8,128]{2,1,0:T(8,128)S(1)}, f32[32,8,128]{2,1,0:T(8,128)S(1)}) custom-call(f32[1,3,16,1024]{3,2,1,0:T(8,128)} %guess_hbm.1, f32[8,3,16,1024]{3,2,1,0:T(8,128)} %forcing_hbm.1, f32[16,1024]{1,0:T(8,128)} %depth_hbm.1, ...), custom_call_target="tpu_custom_call" | custom-call | tf_op jit(solution)/shard_map/pallas_call | solution.py:687
  37.1 4.3 %shard_map.60 = (f32[8,3,16,1024]{3,2,1,0:T(8,128)}, f32[1,3,16,1024]{3,2,1,0:T(8,128)}) custom-call(f32[8,3,32,8,128]{4,3,2,1,0:T(8,128)S(1)} %get-tuple-element.7.track, f32[3,32,8,128]{3,2,1,0:T(8,128)S(1)} %get-tuple-element.8.corrected, f32[3,16,8,128]{3,2,1,0:T(8,128)S(1)} %get-tuple-element.9.own_part, ...), custom_call_target="tpu_custom_call" | custom-call | tf_op jit(solution)/shard_map/pallas_call | solution.py:759
